TPU v7x, 32 devices: a whole 2x2x4 slice. The times are simulated.
32 devices in a mesh: grp: 4 (over z), seq: 8 (over y, x, core).
Axes of the slice: x: 2, y: 2, z: 4, core: 2. Of those that a mesh axis runs over, the one named last changes fastest.
Arguments:
- fine_rows: bfloat16 [4, 1024, 2048], P('grp', 'seq'), may hold values from -6 to 6
- segment_ids: int32 [4, 1024], P('grp', 'seq'), may hold values from 0 to 7, as said below
- pool_gain: float32 [2048], replicated, may hold values from 0.1 to 1.9
- w_in: bfloat16 [2048, 8192], P('grp', 'seq'), may hold values from -0.125 to 0.125
- w_gate: bfloat16 [8192, 16384], P('grp', 'seq'), may hold values from -0.0625 to 0.0625
- w_up: bfloat16 [8192, 16384], P('grp', 'seq'), may hold values from -0.0625 to 0.0625
- w_down: bfloat16 [16384, 8192], P('seq', 'grp'), may hold values from -0.046875 to 0.046875
- out_grad: bfloat16 [4, 64, 8192], P('grp'), may hold values from -6 to 6
Outputs:
- coarse_out: bfloat16 [4, 64, 8192], P('grp', None, 'seq')
- fine_grad: bfloat16 [4, 1024, 2048], P('grp', 'seq')
Inputs may be any that keep to these rules, and one draw needn't show every extreme that they name: `segment_ids`: within each shard of 128 consecutive bytes the numbers count the shard's segments from 0 upward, never falling, every segment one byte or more; a shard holds 4 to 8 segments, some shard of every document exactly 8, and every document 48 segments in all.
All inputs are finite; a program needn't handle non-finite values.
Results may differ from a plain program's by a relative error of at most 0.02.
Values may be sent and summed in bfloat16 or wider, within the bound.
A program may use at most 192 MiB of HBM per device.

v0:
```python
import jax
import jax.numpy as jnp
from jax import lax
from jax.sharding import PartitionSpec as P

SEG_CAP = 8
norm_eps = 1e-06
bf16 = jnp.bfloat16
f32 = jnp.float32


def silu_parts(gate_value):
    sigma = jax.nn.sigmoid(gate_value)
    return (gate_value * sigma, sigma * (1.0 + gate_value * (1.0 - sigma)))


def matmul(a, b):
    return jnp.dot(a, b, preferred_element_type=f32)


def matmul_t(a, b):
    return lax.dot_general(a, b, (((1,), (1,)), ((), ())), preferred_element_type=f32)


def swap_pairs(grps, seqs):
    halves = seqs // grps
    return [
        (g * seqs + p * halves + h, p * seqs + g * halves + h)
        for g in range(grps)
        for p in range(grps)
        for h in range(halves)
    ]


def grp_total(partial_value):
    return lax.psum_scatter(
        partial_value.astype(bf16), "grp", scatter_dimension=0, tiled=True
    ).astype(f32)


def make_shards(grps, seqs):
    halves = seqs // grps
    pairs = swap_pairs(grps, seqs)

    def swap(value):
        return lax.ppermute(value, ("grp", "seq"), pairs)

    def shards(fine_rows, segment_ids, pool_gain, w_in, w_gate, w_up, w_down, out_grad):
        rows_here = fine_rows[0]
        index_here = segment_ids[0]
        feat, width = w_in.shape
        slots = jnp.arange(SEG_CAP, dtype=jnp.int32)
        member = index_here[None, :] == slots[:, None]
        segment_sums = matmul(member.astype(bf16), rows_here)
        inv_rms = lax.rsqrt(jnp.mean(segment_sums * segment_sums, axis=1, keepdims=True) + norm_eps)
        pooled = (segment_sums * inv_rms * pool_gain).astype(bf16)
        live_count = jnp.max(index_here) + 1
        packed = jnp.concatenate(
            [pooled, jnp.full((1, pooled.shape[1]), live_count.astype(bf16))], axis=0
        )
        gathered = lax.all_gather(packed, "seq", axis=0)
        shard_counts = gathered[:, SEG_CAP, 0].astype(jnp.int32)
        gathered = gathered[:, :SEG_CAP].reshape(seqs * SEG_CAP, -1)
        offsets = jnp.cumsum(shard_counts) - shard_counts
        slot_count = seqs * SEG_CAP
        within = jnp.tile(slots, seqs)
        target = jnp.repeat(offsets, SEG_CAP) + within
        is_live = within < jnp.repeat(shard_counts, SEG_CAP)
        rows = slot_count * 3 // 4
        select = (target[None, :] == jnp.arange(rows, dtype=jnp.int32)[:, None]) & is_live[None, :]
        selector = select.astype(bf16)
        work_in = matmul(selector, gathered).astype(bf16)
        work_in = lax.all_to_all(
            work_in.reshape(rows, grps, feat), "grp", split_axis=1, concat_axis=0
        ).reshape(grps * rows, feat)
        x_cols = grp_total(matmul(work_in, w_in)).astype(bf16)
        seq_at = lax.axis_index("seq")
        block = w_gate.shape[0]
        piece = block // seqs
        grad_here = out_grad[0].reshape(slot_count, grps, seqs, piece)
        grad_part = lax.dynamic_index_in_dim(grad_here, seq_at, 2, keepdims=False)
        grad_part = matmul(selector, grad_part.reshape(slot_count, grps * piece)).astype(bf16)
        grad_part = lax.all_to_all(
            grad_part.reshape(rows, grps, piece), "grp", split_axis=1, concat_axis=0
        ).reshape(grps * rows, piece)
        work_grad = lax.all_gather(grad_part, "seq", axis=1, tiled=True)
        grad_hidden = grp_total(matmul_t(work_grad, w_down))

        def spread(cols):
            every = lax.all_gather(swap(cols), "seq", axis=0)
            every = every.reshape(grps, halves, rows, width)
            return every.transpose(0, 2, 1, 3).reshape(grps * rows, halves * width)

        def column_total(part):
            part = part.astype(bf16).reshape(grps, rows, halves, width)
            part = part.transpose(0, 2, 1, 3).reshape(seqs * rows, width)
            return swap(lax.psum_scatter(part, "seq", scatter_dimension=0, tiled=True)).astype(f32)

        coarse_x = spread(x_cols)
        gate_value = grp_total(matmul(coarse_x, w_gate))
        up_value = grp_total(matmul(coarse_x, w_up))
        activated, derivative = silu_parts(gate_value)
        hidden = (activated * up_value).astype(bf16)
        grad_gate = (grad_hidden * up_value * derivative).astype(bf16)
        grad_up = (grad_hidden * activated).astype(bf16)
        grad_gate = lax.all_gather(grad_gate, "grp", axis=0, tiled=True)
        grad_up = lax.all_gather(grad_up, "grp", axis=0, tiled=True)
        hidden = lax.all_gather(hidden, "grp", axis=0, tiled=True)
        back_cols = column_total(matmul_t(grad_gate, w_gate) + matmul_t(grad_up, w_up))
        down_cols = column_total(matmul(hidden, w_down))
        out_cols = (x_cols.astype(f32) + down_cols).astype(bf16)
        out_cols = matmul(selector.T, out_cols).astype(bf16)
        grad_cols = lax.dynamic_slice_in_dim(out_grad[0], seq_at * width, width, 1)
        grad_cols = matmul(selector, grad_cols)
        grad_x = (back_cols + grad_cols).astype(bf16)
        grad_x = lax.all_gather(grad_x, "grp", axis=0, tiled=True)
        term = matmul_t(grad_x, w_in).astype(bf16)
        term = lax.all_to_all(
            term.reshape(grps, rows, feat), "grp", split_axis=0, concat_axis=1
        ).reshape(rows, grps * feat)
        term = matmul(selector.T, term).astype(bf16)
        grad_pooled = lax.psum_scatter(term, "seq", scatter_dimension=0, tiled=True).astype(f32)
        weighted = grad_pooled * pool_gain
        inner = jnp.mean(weighted * segment_sums, axis=1, keepdims=True)
        grad_sums = inv_rms * weighted - segment_sums * (inv_rms * inv_rms * inv_rms) * inner
        fine_grad = matmul(member.astype(bf16).T, grad_sums.astype(bf16)).astype(bf16)
        return (out_cols[None], fine_grad[None])

    return shards


def solution(mesh):
    return jax.shard_map(
        make_shards(mesh.shape["grp"], mesh.shape["seq"]),
        mesh=mesh,
        in_specs=(
            P("grp", "seq", None),
            P("grp", "seq"),
            P(),
            P("grp", "seq"),
            P("grp", "seq"),
            P("grp", "seq"),
            P("seq", "grp"),
            P("grp", None, None),
        ),
        out_specs=(P("grp", None, "seq"), P("grp", "seq", None)),
        check_vma=False,
    )
```

profile of v0, /device:TPU:0, one launch (start us, length us, event | category | flops | bytes accessed | tf_op | source)
XLA Modules:
  0.0 326.0 jit_solution(11023302746642176019)
XLA Ops:
  7.2 1.4 multiply_reduce_fusion.1
  8.6 1.3 reduce_max.9
  10.6 0.8 multiply_convert_fusion
  11.4 11.3 %all-gather.2 = bf16[8,9,2048]{2,1,0:T(8,128)(2,1)S(1)} all-gather(bf16[1,9,2048]{2,1,0:T(8,128)(2,1)S(1)} %pad_bitcast_fusion), channel_id=2, replica_groups=mesh['grp'=4,'seq'=8] {'seq'}, dimensions={0}, use_global_device_ids=true | all-gather | bytes 331776 | tf_op jit(solution)/shard_map/all_gather | solution.py:61
  22.7 0.2 fusion.39
  22.9 0.1 iota_compare_fusion.1
  23.0 0.2 reduce-window.9
  23.2 0.1 iota_add_fusion
  23.3 0.1 add.65
  23.4 0.1 lt.18
  23.4 0.2 convolution_convert_fusion.6
  23.6 0.1 broadcast_in_dim_reshape.9
  23.8 0.7 copy.18
  24.5 4.9 %all-to-all-start = ((bf16[1,48,4,512]{3,1,0,2:T(8,128)(2,1)}), bf16[1,48,4,512]{3,1,0,2:T(8,128)(2,1)S(1)}, u32[]{:S(2)}, u32[]{:S(2)}) async-start(bf16[1,48,4,512]{3,1,0,2:T(8,128)(2,1)} %copy.18), calls=%async_computation | async-start | bytes 393216 | tf_op jit(solution)/shard_map/all_to_all | solution.py:73
  29.4 1.5 copy.28
  30.9 0.8 dynamic-slice_reduce_fusion
  31.7 0.2 convolution_convert_fusion.10
  31.9 0.1 broadcast_in_dim_reshape.10
  31.9 0.7 copy.22
  32.6 4.8 %all-to-all-done = bf16[1,48,4,512]{3,1,0,2:T(8,128)(2,1)S(1)} async-done(((bf16[1,48,4,512]{3,1,0,2:T(8,128)(2,1)}), bf16[1,48,4,512]{3,1,0,2:T(8,128)(2,1)S(1)}, u32[]{:S(2)}, u32[]{:S(2)}) %all-to-all-start) | async-done | bytes 196640 | tf_op jit(solution)/shard_map/all_to_all | solution.py:73
  37.4 3.3 %all-to-all-start.1 = ((bf16[1,48,4,256]{3,1,0,2:T(8,128)(2,1)}), bf16[1,48,4,256]{3,1,0,2:T(8,128)(2,1)S(1)}, u32[]{:S(2)}, u32[]{:S(2)}) async-start(bf16[1,48,4,256]{3,1,0,2:T(8,128)(2,1)} %copy.22), calls=%async_computation.5 | async-start | bytes 196608 | tf_op jit(solution)/shard_map/all_to_all | solution.py:83
  40.7 0.0 reduce-scatter.8.cloned.1.call-start
  40.7 1.1 convolution_convert_fusion.7
  41.9 0.0 reduce-scatter.16.cloned.1.call-start
  41.9 4.5 %all-to-all-done.1 = bf16[1,48,4,256]{3,1,0,2:T(8,128)(2,1)S(1)} async-done(((bf16[1,48,4,256]{3,1,0,2:T(8,128)(2,1)}), bf16[1,48,4,256]{3,1,0,2:T(8,128)(2,1)S(1)}, u32[]{:S(2)}, u32[]{:S(2)}) %all-to-all-start.1) | async-done | bytes 98336 | tf_op jit(solution)/shard_map/all_to_all | solution.py:83
  46.5 11.9 %all_gather.32 = bf16[192,2048]{1,0:T(8,128)(2,1)S(1)} all-gather(bf16[192,256]{1,0:T(8,128)(2,1)S(1)} %bitcast.93), channel_id=1, replica_groups=mesh['grp'=4,'seq'=8] {'seq'}, dimensions={1}, use_global_device_ids=true | all-gather | bytes 884736 | tf_op jit(solution)/shard_map/all_gather | solution.py:86
  58.4 7.2 %convolution_convert_fusion = bf16[192,2048]{1,0:T(8,128)(2,1)} fusion(bf16[192,2048]{1,0:T(8,128)(2,1)S(1)} %all_gather.32, bf16[2048,2048]{1,0:T(8,128)(2,1)} %param.14), kind=kOutput, calls=%fused_computation.1 | convolution fusion | flops 1611005952 | bytes 9961472 | tf_op jit(solution)/shard_map/dot_general | solution.py:22
  65.7 1.6 collective-permute-start
  67.3 27.1 %all-gather.1 = bf16[384,1024]{1,0:T(8,128)(2,1)S(1)} all-gather(bf16[48,1024]{1,0:T(8,128)(2,1)S(1)} %collective-permute-done), channel_id=3, replica_groups=mesh['grp'=4,'seq'=8] {'seq'}, dimensions={0}, use_global_device_ids=true | all-gather | bytes 884736 | tf_op jit(solution)/shard_map/all_gather | solution.py:90
  94.4 0.8 copy.19
  95.3 0.2 copy.27
  95.5 6.1 %convolution_convert_fusion.3 = bf16[192,2048]{1,0:T(8,128)(2,1)} fusion(bf16[192,2048]{1,0:T(8,128)(2,1)S(1)} %bitcast.87, bf16[2048,2048]{1,0:T(8,128)(2,1)} %param.12), kind=kOutput, calls=%fused_computation.4 | convolution fusion | flops 1611005952 | bytes 9961472 | tf_op jit(solution)/shard_map/dot_general | solution.py:18
  101.6 0.0 reduce-scatter.12.cloned.1.call-start
  101.6 6.1 %convolution_convert_fusion.2 = bf16[192,2048]{1,0:T(8,128)(2,1)} fusion(bf16[192,2048]{1,0:T(8,128)(2,1)S(1)} %bitcast.88, bf16[2048,2048]{1,0:T(8,128)(2,1)} %param.13), kind=kOutput, calls=%fused_computation.3 | convolution fusion | flops 1611005952 | bytes 9961472 | tf_op jit(solution)/shard_map/dot_general | solution.py:18
  107.7 0.0 reduce-scatter.18.cloned.1.call-start
  107.8 14.5 %reduce-scatter.10.cloned.1.call-done = bf16[48,2048]{1,0:T(8,128)(2,1)} async-done(((bf16[192,2048]{1,0:T(8,128)(2,1)}), bf16[48,2048]{1,0:T(8,128)(2,1)}) %reduce-scatter.10.cloned.1.call-update) | async-done | bytes 196624 | tf_op jit(solution)/shard_map/reduce_scatter | solution.py:36
  122.3 24.9 %reduce-scatter.12.cloned.1.call-done = bf16[48,2048]{1,0:T(8,128)(2,1)} async-done(((bf16[192,2048]{1,0:T(8,128)(2,1)}), bf16[48,2048]{1,0:T(8,128)(2,1)}) %reduce-scatter.12.cloned.1.call-update) | async-done | bytes 196624 | tf_op jit(solution)/shard_map/reduce_scatter | solution.py:36
  147.1 1.4 fusion.8
  148.5 18.2 %all_gather.33 = bf16[192,2048]{1,0:T(8,128)(2,1)S(1)} all-gather(bf16[48,2048]{1,0:T(8,128)(2,1)S(1)} %get-tuple-element.3), channel_id=1, replica_groups=mesh['grp'=4,'seq'=8] {'grp'}, dimensions={0}, use_global_device_ids=true | all-gather | bytes 983040 | tf_op jit(solution)/shard_map/all_gather | solution.py:106
  166.7 6.3 %fusion.43 = f32[192,2048]{1,0:T(8,128)S(1)} fusion(bf16[192,2048]{1,0:T(8,128)(2,1)S(1)} %all_gather.33, bf16[2048,2048]{1,0:T(8,128)(2,1)} %param.12), kind=kOutput, calls=%fused_computation.73 | convolution fusion | flops 1610612736 | bytes 10747904 | tf_op jit(solution)/shard_map/dot_general | solution.py:22
  173.0 17.4 %all_gather.34 = bf16[192,2048]{1,0:T(8,128)(2,1)S(1)} all-gather(bf16[48,2048]{1,0:T(8,128)(2,1)S(1)} %get-tuple-element.2), channel_id=1, replica_groups=mesh['grp'=4,'seq'=8] {'grp'}, dimensions={0}, use_global_device_ids=true | all-gather | bytes 983040 | tf_op jit(solution)/shard_map/all_gather | solution.py:107
  190.4 6.3 %fusion = bf16[192,2048]{1,0:T(8,128)(2,1)S(1)} fusion(f32[192,2048]{1,0:T(8,128)S(1)} %fusion.43, bf16[192,2048]{1,0:T(8,128)(2,1)S(1)} %all_gather.34, bf16[2048,2048]{1,0:T(8,128)(2,1)} %param.13), kind=kOutput, calls=%fused_computation.5 | convolution fusion | flops 1611399168 | bytes 11534336 | tf_op jit(solution)/shard_map/dot_general | solution.py:22
  196.7 0.6 reshape.115
  197.2 1.1 copy.23
  198.4 0.0 reduce-scatter.14.cloned.1.call-start
  198.4 16.8 %all_gather.31 = bf16[192,2048]{1,0:T(8,128)(2,1)S(1)} all-gather(bf16[48,2048]{1,0:T(8,128)(2,1)S(1)} %get-tuple-element.4), channel_id=1, replica_groups=mesh['grp'=4,'seq'=8] {'grp'}, dimensions={0}, use_global_device_ids=true | all-gather | bytes 983040 | tf_op jit(solution)/shard_map/all_gather | solution.py:108
  215.2 18.1 %reduce-scatter.18.cloned.1.call-done = bf16[48,1024]{1,0:T(8,128)(2,1)} async-done(((bf16[384,1024]{1,0:T(8,128)(2,1)}), bf16[48,1024]{1,0:T(8,128)(2,1)}) %reduce-scatter.18.cloned.1.call-update) | async-done | bytes 98320 | tf_op jit(solution)/shard_map/reduce_scatter | solution.py:97
  233.4 1.5 collective-permute-start.2
  234.9 5.2 %convolution_convert_fusion.1 = bf16[192,2048]{1,0:T(8,128)(2,1)S(1)} fusion(bf16[192,2048]{1,0:T(8,128)(2,1)S(1)} %all_gather.31, bf16[2048,2048]{1,0:T(8,128)(2,1)} %param.14), kind=kOutput, calls=%fused_computation.2 | convolution fusion | flops 1611005952 | bytes 9961472 | tf_op jit(solution)/shard_map/dot_general | solution.py:18
  240.1 0.6 reshape.112
  240.7 1.1 copy.20
  241.8 0.0 reduce-scatter.20.cloned.1.call-start
  241.9 1.1 add_convert_fusion
  243.0 16.2 %all_gather.35 = bf16[192,1024]{1,0:T(8,128)(2,1)S(1)} all-gather(bf16[48,1024]{1,0:T(8,128)(2,1)S(1)} %add_convert_fusion), channel_id=1, replica_groups=mesh['grp'=4,'seq'=8] {'grp'}, dimensions={0}, use_global_device_ids=true | all-gather | bytes 491520 | tf_op jit(solution)/shard_map/all_gather | solution.py:116
  259.1 0.5 convolution_convert_fusion.8
  259.6 11.9 %all_to_all.45 = bf16[4,48,1,512]{3,1,2,0:T(8,128)(2,1)S(1)} all-to-all(bf16[4,48,1,512]{3,1,2,0:T(8,128)(2,1)S(1)} %bitcast.85), channel_id=1, replica_groups=mesh['grp'=4,'seq'=8] {'grp'}, dimensions={0} | all-to-all | bytes 393216 | tf_op jit(solution)/shard_map/all_to_all | solution.py:118
  271.5 0.2 copy.25
  271.7 1.0 convolution_convert_fusion.5
  272.7 6.1 %reduce-scatter.14.cloned.1.call-done = bf16[48,1024]{1,0:T(8,128)(2,1)} async-done(((bf16[384,1024]{1,0:T(8,128)(2,1)}), bf16[48,1024]{1,0:T(8,128)(2,1)}) %reduce-scatter.14.cloned.1.call-update) | async-done | bytes 98320 | tf_op jit(solution)/shard_map/reduce_scatter | solution.py:97
  278.8 1.5 collective-permute-start.1
  280.3 0.9 fusion.2
  281.2 35.1 %reduce-scatter.20.cloned.1.call-done = bf16[8,2048]{1,0:T(8,128)(2,1)} async-done(((bf16[64,2048]{1,0:T(8,128)(2,1)}), bf16[8,2048]{1,0:T(8,128)(2,1)}) %reduce-scatter.20.cloned.1.call-update) | async-done | bytes 32784 | tf_op jit(solution)/shard_map/reduce_scatter | solution.py:122
  316.3 0.9 multiply_reduce_fusion
  317.2 1.9 fusion.1
  (27 shorter events, 0.3 us)
Async XLA Ops:
  7.2 33.6 %copy-start = (bf16[512,1024]{1,0:T(8,128)(2,1)S(1)}, bf16[512,1024]{1,0:T(8,128)(2,1)}, u32[]{:S(2)}) copy-start(bf16[512,1024]{1,0:T(8,128)(2,1)} %param.11) | copy-start | bytes 3145732
  24.5 12.9 %all-to-all-start = ((bf16[1,48,4,512]{3,1,0,2:T(8,128)(2,1)}), bf16[1,48,4,512]{3,1,0,2:T(8,128)(2,1)S(1)}, u32[]{:S(2)}, u32[]{:S(2)}) async-start(bf16[1,48,4,512]{3,1,0,2:T(8,128)(2,1)} %copy.18), calls=%async_computation | async-start | bytes 393216 | tf_op jit(solution)/shard_map/all_to_all | solution.py:73
  37.4 9.1 %all-to-all-start.1 = ((bf16[1,48,4,256]{3,1,0,2:T(8,128)(2,1)}), bf16[1,48,4,256]{3,1,0,2:T(8,128)(2,1)S(1)}, u32[]{:S(2)}, u32[]{:S(2)}) async-start(bf16[1,48,4,256]{3,1,0,2:T(8,128)(2,1)} %copy.22), calls=%async_computation.5 | async-start | bytes 196608 | tf_op jit(solution)/shard_map/all_to_all | solution.py:83
  40.7 25.1 %reduce-scatter.8.cloned.1.call-start = ((), (), s32[]{:S(2)}) async-start(), calls=%async_computation.10 | async-start | bytes 491520 | tf_op jit(solution)/shard_map/reduce_scatter | solution.py:36
  41.9 65.9 %reduce-scatter.16.cloned.1.call-start = ((), (), s32[]{:S(2)}) async-start(), calls=%async_computation.14 | async-start | bytes 983040 | tf_op jit(solution)/shard_map/reduce_scatter | solution.py:36
  65.7 56.6 %reduce-scatter.10.cloned.1.call-start = ((), (), s32[]{:S(2)}) async-start(), calls=%async_computation.11 | async-start | bytes 983040 | tf_op jit(solution)/shard_map/reduce_scatter | solution.py:36
  65.7 1.6 collective-permute-start
  101.6 45.6 %reduce-scatter.12.cloned.1.call-start = ((), (), s32[]{:S(2)}) async-start(), calls=%async_computation.12 | async-start | bytes 983040 | tf_op jit(solution)/shard_map/reduce_scatter | solution.py:36
  107.7 125.6 %reduce-scatter.18.cloned.1.call-start = ((), (), s32[]{:S(2)}) async-start(), calls=%async_computation.15 | async-start | bytes 884736 | tf_op jit(solution)/shard_map/reduce_scatter | solution.py:97
  198.4 80.4 %reduce-scatter.14.cloned.1.call-start = ((), (), s32[]{:S(2)}) async-start(), calls=%async_computation.13 | async-start | bytes 884736 | tf_op jit(solution)/shard_map/reduce_scatter | solution.py:97
  215.2 65.1 %copy-start.1 = (bf16[48,1024]{1,0:T(8,128)(2,1)S(1)}, bf16[48,1024]{1,0:T(8,128)(2,1)}, u32[]{:S(2)}) copy-start(bf16[48,1024]{1,0:T(8,128)(2,1)} %reduce-scatter.8.cloned.1.call-done) | copy-start | bytes 294916
  233.4 8.5 %collective-permute-start.2 = (bf16[48,1024]{1,0:T(8,128)(2,1)}, bf16[48,1024]{1,0:T(8,128)(2,1)S(1)}, u32[]{:S(2)}, u32[]{:S(2)}) collective-permute-start(bf16[48,1024]{1,0:T(8,128)(2,1)} %reduce-scatter.18.cloned.1.call-done), channel_id=1, source_target_pairs={{0,0},{1,1},{2,8},{3,9},{4,16},{5,17},{6,24},{7,25},{8,2},{9,3},{1... | collective-permute-start | bytes 294920 | tf_op jit(solution)/shard_map/ppermute | solution.py:46
  240.1 76.2 %copy-start.2 = (f32[2048]{0:T(1024)S(1)}, f32[2048]{0:T(1024)}, u32[]{:S(2)}) copy-start(f32[2048]{0:T(1024)} %param.10) | copy-start | bytes 24580
  240.1 77.1 %copy-start.3 = (s32[1,128]{1,0:T(1,128)S(1)}, s32[1,128]{1,0:T(1,128)}, u32[]{:S(2)}) copy-start(s32[1,128]{1,0:T(1,128)} %param.9) | copy-start | bytes 1540
  241.8 74.5 %reduce-scatter.20.cloned.1.call-start = ((), (), s32[]{:S(2)}) async-start(), calls=%async_computation.16 | async-start | bytes 294912 | tf_op jit(solution)/shard_map/reduce_scatter | solution.py:122
  278.8 1.5 collective-permute-start.1
Sparse Core Ops, SparseCore 0:
  44.4 21.0 reduce-scatter.7
  67.8 26.4 reduce-scatter.15
  101.7 20.5 reduce-scatter.9
  124.5 22.5 reduce-scatter.11
  198.5 34.8 reduce-scatter.17
  242.0 36.7 reduce-scatter.13
  282.7 33.5 reduce-scatter.19
where the time goes:
time: 327 us; the launch traced here: 326 us
  blocking collectives  131 us (40%)
  waiting for transfers between devices  108 us (33%)
  matrix products  45.5 us (14%)
  between operations  15 us (5%)
  starting transfers between devices  13.1 us (4%)
  local copies, waits for them, and re-layouts  8.58 us (3%)
  other arithmetic  4.91 us (2%)
    reduce_scatter x4, waiting for transfers between devices, grp_total(): lax.psum_scatter(partial_value.astype(bf16), 'grp', scatter_dimension=0,...  39.4 us
    reduce_scatter x1, waiting for transfers between devices, shards(): lax.psum_scatter(term, 'seq', scatter_dimension=0, tiled=True).astype(f32)  35.1 us
    all_gather x1, blocking collectives, spread(): every = lax.all_gather(swap(cols), 'seq', axis=0)  27.1 us
    dot_general x11, matrix products, matmul(): return jnp.dot(a, b, preferred_element_type=f32)  25.2 us
    reduce_scatter x2, waiting for transfers between devices, column_total(): lax.psum_scatter(part, 'seq', scatter_dimension=0, tiled=True)  24.2 us
    dot_general x4, matrix products, matmul_t(): lax.dot_general(a, b, (((1,), (1,)), ((), ())), preferred_element_type=f32)  20.3 us
    all_gather x1, blocking collectives, shards(): grad_gate = lax.all_gather(grad_gate, 'grp', axis=0, tiled=True)  18.2 us
    all_gather x1, blocking collectives, shards(): grad_up = lax.all_gather(grad_up, 'grp', axis=0, tiled=True)  17.4 us
  transfers between devices with their start and end apart: 12, of which 7 were waited for; matrix products, arithmetic and copies ran while one was open for 11% of the time, Pallas kernels for 0%

commit v1 on v0

--- a/solution.py
+++ b/solution.py
@@ -7,6 +7,16 @@
 norm_eps = 1e-06
 bf16 = jnp.bfloat16
 f32 = jnp.float32
+
+
+def ends_perform(patch, at_axis):
+    patch = jnp.moveaxis(patch, 0, at_axis)
+    current_value = patch.shape
+    return patch.reshape(
+        *current_value[:at_axis],
+        current_value[at_axis] * current_value[at_axis + 1],
+        *current_value[at_axis + 2 :]
+    )
 
 
 def silu_parts(gate_value):
@@ -113,7 +123,15 @@
         grad_cols = lax.dynamic_slice_in_dim(out_grad[0], seq_at * width, width, 1)
         grad_cols = matmul(selector, grad_cols)
         grad_x = (back_cols + grad_cols).astype(bf16)
-        grad_x = lax.all_gather(grad_x, "grp", axis=0, tiled=True)
+        axis_len = lax.axis_size("grp")
+        inbox = [(dev_j, (dev_j + 1) % axis_len) for dev_j in range(axis_len)]
+        kept_rows = [grad_x]
+        while len(kept_rows) < axis_len:
+            kept_rows.append(lax.ppermute(kept_rows[-1], "grp", inbox))
+        mixed_arr = lax.axis_index("grp")
+        state_now = jnp.stack(kept_rows, axis=0)
+        kept_rows = state_now[(mixed_arr - jnp.arange(axis_len)) % axis_len]
+        grad_x = ends_perform(kept_rows, 0)
         term = matmul_t(grad_x, w_in).astype(bf16)
         term = lax.all_to_all(
             term.reshape(grps, rows, feat), "grp", split_axis=0, concat_axis=1

time: 327 us -> 354 us (1.083)
  waiting for transfers between devices: 108 us -> 141 us
  blocking collectives: 131 us -> 122 us
    reduce_scatter x2, waiting for transfers between devices: 24.2 us -> 46.1 us  [column_total(): lax.psum_scatter(part, 'seq', scatter_dimension=0, tiled=True)]
    all_gather x1 -> x0, blocking collectives: 16.2 us -> none  [shards(): grad_x = lax.all_gather(grad_x, 'grp', axis=0, tiled=True)]
    ppermute x0 -> x3, waiting for transfers between devices: none -> 11.6 us  [shards(): kept_rows.append(lax.ppermute(kept_rows[-1], 'grp', inbox))]
    all_gather x1, blocking collectives: 16.8 us -> 26.6 us  [shards(): hidden = lax.all_gather(hidden, 'grp', axis=0, tiled=True)]
  transfers between devices with their start and end apart: 12 -> 15, of which waited for: 7 -> 9; matrix products, arithmetic and copies ran while one was open for 11% -> 10% of each run, Pallas kernels for 0% -> 0%
where the time goes in v1:
time: 354 us; the launch traced here: 353 us
  waiting for transfers between devices  141 us (40%)
  blocking collectives  122 us (34%)
  matrix products  45.5 us (13%)
  between operations  15 us (4%)
  starting transfers between devices  14.8 us (4%)
  local copies, waits for them, and re-layouts  9.15 us (3%)
  other arithmetic  4.98 us (1%)
    reduce_scatter x2, waiting for transfers between devices, column_total(): lax.psum_scatter(part, 'seq', scatter_dimension=0, tiled=True)  46.1 us
    reduce_scatter x4, waiting for transfers between devices, grp_total(): lax.psum_scatter(partial_value.astype(bf16), 'grp', scatter_dimension=0,...  39.4 us
    reduce_scatter x1, waiting for transfers between devices, shards(): lax.psum_scatter(term, 'seq', scatter_dimension=0, tiled=True).astype(f32)  35.1 us
    all_gather x1, blocking collectives, spread(): every = lax.all_gather(swap(cols), 'seq', axis=0)  27.1 us
    all_gather x1, blocking collectives, shards(): hidden = lax.all_gather(hidden, 'grp', axis=0, tiled=True)  26.6 us
    dot_general x11, matrix products, matmul(): return jnp.dot(a, b, preferred_element_type=f32)  25.2 us
    dot_general x4, matrix products, matmul_t(): lax.dot_general(a, b, (((1,), (1,)), ((), ())), preferred_element_type=f32)  20.3 us
    all_gather x1, blocking collectives, shards(): grad_gate = lax.all_gather(grad_gate, 'grp', axis=0, tiled=True)  18.2 us
  transfers between devices with their start and end apart: 15, of which 9 were waited for; matrix products, arithmetic and copies ran while one was open for 10% of the time, Pallas kernels for 0%

profile of v1, /device:TPU:0, one launch (start us, length us, event | category | flops | bytes accessed | tf_op | source)
XLA Modules:
  0.0 352.6 jit_solution(3769620022178258324)
XLA Ops:
  7.2 1.4 multiply_reduce_fusion.1
  8.6 1.3 reduce_max.9
  10.6 0.8 multiply_convert_fusion
  11.4 11.3 %all-gather.2 = bf16[8,9,2048]{2,1,0:T(8,128)(2,1)S(1)} all-gather(bf16[1,9,2048]{2,1,0:T(8,128)(2,1)S(1)} %pad_bitcast_fusion), channel_id=2, replica_groups=mesh['grp'=4,'seq'=8] {'seq'}, dimensions={0}, use_global_device_ids=true | all-gather | bytes 331776 | tf_op jit(solution)/shard_map/all_gather | solution.py:71
  22.7 0.2 fusion.39
  22.9 0.1 iota_compare_fusion.1
  23.0 0.2 reduce-window.9
  23.2 0.1 iota_add_fusion
  23.3 0.1 add.88
  23.4 0.1 lt.34
  23.4 0.2 convolution_convert_fusion.6
  23.6 0.1 broadcast_in_dim_reshape.9
  23.8 0.7 copy.19
  24.5 4.9 %all-to-all-start = ((bf16[1,48,4,512]{3,1,0,2:T(8,128)(2,1)}), bf16[1,48,4,512]{3,1,0,2:T(8,128)(2,1)S(1)}, u32[]{:S(2)}, u32[]{:S(2)}) async-start(bf16[1,48,4,512]{3,1,0,2:T(8,128)(2,1)} %copy.19), calls=%async_computation | async-start | bytes 393216 | tf_op jit(solution)/shard_map/all_to_all | solution.py:83
  29.4 1.5 copy.29
  30.9 0.8 dynamic-slice_reduce_fusion
  31.7 0.2 convolution_convert_fusion.10
  31.9 0.1 broadcast_in_dim_reshape.10
  31.9 0.7 copy.23
  32.6 4.8 %all-to-all-done = bf16[1,48,4,512]{3,1,0,2:T(8,128)(2,1)S(1)} async-done(((bf16[1,48,4,512]{3,1,0,2:T(8,128)(2,1)}), bf16[1,48,4,512]{3,1,0,2:T(8,128)(2,1)S(1)}, u32[]{:S(2)}, u32[]{:S(2)}) %all-to-all-start) | async-done | bytes 196640 | tf_op jit(solution)/shard_map/all_to_all | solution.py:83
  37.4 3.3 all-to-all-start.1
  40.7 0.0 reduce-scatter.8.cloned.1.call-start
  40.7 1.1 convolution_convert_fusion.7
  41.9 4.5 %all-to-all-done.1 = bf16[1,48,4,256]{3,1,0,2:T(8,128)(2,1)S(1)} async-done(((bf16[1,48,4,256]{3,1,0,2:T(8,128)(2,1)}), bf16[1,48,4,256]{3,1,0,2:T(8,128)(2,1)S(1)}, u32[]{:S(2)}, u32[]{:S(2)}) %all-to-all-start.1) | async-done | bytes 98336 | tf_op jit(solution)/shard_map/all_to_all | solution.py:93
  46.5 11.9 %all_gather.29 = bf16[192,2048]{1,0:T(8,128)(2,1)S(1)} all-gather(bf16[192,256]{1,0:T(8,128)(2,1)S(1)} %bitcast.102), channel_id=1, replica_groups=mesh['grp'=4,'seq'=8] {'seq'}, dimensions={1}, use_global_device_ids=true | all-gather | bytes 884736 | tf_op jit(solution)/shard_map/all_gather | solution.py:96
  58.4 7.2 %convolution_convert_fusion = bf16[192,2048]{1,0:T(8,128)(2,1)} fusion(bf16[192,2048]{1,0:T(8,128)(2,1)S(1)} %all_gather.29, bf16[2048,2048]{1,0:T(8,128)(2,1)} %param.14), kind=kOutput, calls=%fused_computation.2 | convolution fusion | flops 1611005952 | bytes 9961472 | tf_op jit(solution)/shard_map/dot_general | solution.py:32
  65.7 1.6 collective-permute-start
  67.3 27.1 %all-gather.1 = bf16[384,1024]{1,0:T(8,128)(2,1)S(1)} all-gather(bf16[48,1024]{1,0:T(8,128)(2,1)S(1)} %collective-permute-done), channel_id=3, replica_groups=mesh['grp'=4,'seq'=8] {'seq'}, dimensions={0}, use_global_device_ids=true | all-gather | bytes 884736 | tf_op jit(solution)/shard_map/all_gather | solution.py:100
  94.4 0.8 copy.20
  95.3 0.2 copy.28
  95.5 6.1 %convolution_convert_fusion.3 = bf16[192,2048]{1,0:T(8,128)(2,1)} fusion(bf16[192,2048]{1,0:T(8,128)(2,1)S(1)} %bitcast.95, bf16[2048,2048]{1,0:T(8,128)(2,1)} %param.12), kind=kOutput, calls=%fused_computation.5 | convolution fusion | flops 1611005952 | bytes 9961472 | tf_op jit(solution)/shard_map/dot_general | solution.py:28
  101.6 6.1 %convolution_convert_fusion.2 = bf16[192,2048]{1,0:T(8,128)(2,1)} fusion(bf16[192,2048]{1,0:T(8,128)(2,1)S(1)} %bitcast.96, bf16[2048,2048]{1,0:T(8,128)(2,1)} %param.13), kind=kOutput, calls=%fused_computation.4 | convolution fusion | flops 1611005952 | bytes 9961472 | tf_op jit(solution)/shard_map/dot_general | solution.py:28
  107.8 14.5 %reduce-scatter.10.cloned.1.call-done = bf16[48,2048]{1,0:T(8,128)(2,1)} async-done(((bf16[192,2048]{1,0:T(8,128)(2,1)}), bf16[48,2048]{1,0:T(8,128)(2,1)}) %reduce-scatter.10.cloned.1.call-update) | async-done | bytes 196624 | tf_op jit(solution)/shard_map/reduce_scatter | solution.py:46
  122.3 24.9 %reduce-scatter.12.cloned.1.call-done = bf16[48,2048]{1,0:T(8,128)(2,1)} async-done(((bf16[192,2048]{1,0:T(8,128)(2,1)}), bf16[48,2048]{1,0:T(8,128)(2,1)}) %reduce-scatter.12.cloned.1.call-update) | async-done | bytes 196624 | tf_op jit(solution)/shard_map/reduce_scatter | solution.py:46
  147.1 1.4 fusion.8
  148.5 18.2 %all_gather.30 = bf16[192,2048]{1,0:T(8,128)(2,1)S(1)} all-gather(bf16[48,2048]{1,0:T(8,128)(2,1)S(1)} %get-tuple-element.3), channel_id=1, replica_groups=mesh['grp'=4,'seq'=8] {'grp'}, dimensions={0}, use_global_device_ids=true | all-gather | bytes 983040 | tf_op jit(solution)/shard_map/all_gather | solution.py:116
  166.7 6.3 %fusion.45 = f32[192,2048]{1,0:T(8,128)S(1)} fusion(bf16[192,2048]{1,0:T(8,128)(2,1)S(1)} %all_gather.30, bf16[2048,2048]{1,0:T(8,128)(2,1)} %param.12), kind=kOutput, calls=%fused_computation.82 | convolution fusion | flops 1610612736 | bytes 10747904 | tf_op jit(solution)/shard_map/dot_general | solution.py:32
  173.0 17.4 %all_gather.31 = bf16[192,2048]{1,0:T(8,128)(2,1)S(1)} all-gather(bf16[48,2048]{1,0:T(8,128)(2,1)S(1)} %get-tuple-element.2), channel_id=1, replica_groups=mesh['grp'=4,'seq'=8] {'grp'}, dimensions={0}, use_global_device_ids=true | all-gather | bytes 983040 | tf_op jit(solution)/shard_map/all_gather | solution.py:117
  190.4 6.3 %fusion = bf16[192,2048]{1,0:T(8,128)(2,1)S(1)} fusion(f32[192,2048]{1,0:T(8,128)S(1)} %fusion.45, bf16[192,2048]{1,0:T(8,128)(2,1)S(1)} %all_gather.31, bf16[2048,2048]{1,0:T(8,128)(2,1)} %param.13), kind=kOutput, calls=%fused_computation.6 | convolution fusion | flops 1611399168 | bytes 11534336 | tf_op jit(solution)/shard_map/dot_general | solution.py:32
  196.7 0.6 reshape.167
  197.2 1.1 copy.24
  198.4 35.0 %reduce-scatter.18.cloned.1.call-done = bf16[48,1024]{1,0:T(8,128)(2,1)} async-done(((bf16[384,1024]{1,0:T(8,128)(2,1)}), bf16[48,1024]{1,0:T(8,128)(2,1)}) %reduce-scatter.18.cloned.1.call-update) | async-done | bytes 98320 | tf_op jit(solution)/shard_map/reduce_scatter | solution.py:107
  233.4 1.5 collective-permute-start.2
  234.9 26.6 %all_gather.28 = bf16[192,2048]{1,0:T(8,128)(2,1)S(1)} all-gather(bf16[48,2048]{1,0:T(8,128)(2,1)S(1)} %get-tuple-element.4), channel_id=1, replica_groups=mesh['grp'=4,'seq'=8] {'grp'}, dimensions={0}, use_global_device_ids=true | all-gather | bytes 983040 | tf_op jit(solution)/shard_map/all_gather | solution.py:118
  261.5 1.1 add_convert_fusion
  262.5 0.1 collective-permute-start.3
  262.6 5.2 %convolution_convert_fusion.1 = bf16[192,2048]{1,0:T(8,128)(2,1)S(1)} fusion(bf16[192,2048]{1,0:T(8,128)(2,1)S(1)} %all_gather.28, bf16[2048,2048]{1,0:T(8,128)(2,1)} %param.14), kind=kOutput, calls=%fused_computation.3 | convolution fusion | flops 1611005952 | bytes 9961472 | tf_op jit(solution)/shard_map/dot_general | solution.py:28
  267.8 0.6 reshape.164
  268.4 1.1 copy.21
  269.6 1.7 collective-permute-start.4
  271.3 5.1 %collective-permute-done.4 = bf16[48,1024]{1,0:T(8,128)(2,1)S(1)} collective-permute-done((bf16[48,1024]{1,0:T(8,128)(2,1)S(1)}, bf16[48,1024]{1,0:T(8,128)(2,1)S(1)}, u32[]{:S(2)}, u32[]{:S(2)}) %collective-permute-start.4) | collective-permute-done | bytes 98336 | tf_op jit(solution)/shard_map/ppermute | solution.py:130
  276.4 6.5 %collective-permute-done.5 = bf16[48,1024]{1,0:T(8,128)(2,1)S(1)} collective-permute-done((bf16[48,1024]{1,0:T(8,128)(2,1)S(1)}, bf16[48,1024]{1,0:T(8,128)(2,1)S(1)}, u32[]{:S(2)}, u32[]{:S(2)}) %collective-permute-start.5) | collective-permute-done | bytes 98336 | tf_op jit(solution)/shard_map/ppermute | solution.py:130
  282.8 0.1 pad_maximum_fusion
  282.9 0.6 gather_fusion
  283.5 0.5 convolution_convert_fusion.8
  284.0 9.2 %all_to_all.45 = bf16[4,48,1,512]{3,1,2,0:T(8,128)(2,1)S(1)} all-to-all(bf16[4,48,1,512]{3,1,2,0:T(8,128)(2,1)S(1)} %bitcast.93), channel_id=1, replica_groups=mesh['grp'=4,'seq'=8] {'grp'}, dimensions={0} | all-to-all | bytes 393216 | tf_op jit(solution)/shard_map/all_to_all | solution.py:136
  293.1 0.2 copy.26
  293.4 1.0 convolution_convert_fusion.5
  294.4 11.1 %reduce-scatter.14.cloned.1.call-done = bf16[48,1024]{1,0:T(8,128)(2,1)} async-done(((bf16[384,1024]{1,0:T(8,128)(2,1)}), bf16[48,1024]{1,0:T(8,128)(2,1)}) %reduce-scatter.14.cloned.1.call-update) | async-done | bytes 98320 | tf_op jit(solution)/shard_map/reduce_scatter | solution.py:107
  305.5 1.5 collective-permute-start.1
  307.0 0.9 fusion.2
  307.9 35.1 %reduce-scatter.20.cloned.1.call-done = bf16[8,2048]{1,0:T(8,128)(2,1)} async-done(((bf16[64,2048]{1,0:T(8,128)(2,1)}), bf16[8,2048]{1,0:T(8,128)(2,1)}) %reduce-scatter.20.cloned.1.call-update) | async-done | bytes 32784 | tf_op jit(solution)/shard_map/reduce_scatter | solution.py:140
  343.0 0.9 multiply_reduce_fusion
  343.9 1.9 fusion.1
  (36 shorter events, 0.5 us)
Async XLA Ops:
  7.2 33.6 %copy-start = (bf16[512,1024]{1,0:T(8,128)(2,1)S(1)}, bf16[512,1024]{1,0:T(8,128)(2,1)}, u32[]{:S(2)}) copy-start(bf16[512,1024]{1,0:T(8,128)(2,1)} %param.11) | copy-start | bytes 3145732
  24.5 12.9 %all-to-all-start = ((bf16[1,48,4,512]{3,1,0,2:T(8,128)(2,1)}), bf16[1,48,4,512]{3,1,0,2:T(8,128)(2,1)S(1)}, u32[]{:S(2)}, u32[]{:S(2)}) async-start(bf16[1,48,4,512]{3,1,0,2:T(8,128)(2,1)} %copy.19), calls=%async_computation | async-start | bytes 393216 | tf_op jit(solution)/shard_map/all_to_all | solution.py:83
  37.4 9.1 %all-to-all-start.1 = ((bf16[1,48,4,256]{3,1,0,2:T(8,128)(2,1)}), bf16[1,48,4,256]{3,1,0,2:T(8,128)(2,1)S(1)}, u32[]{:S(2)}, u32[]{:S(2)}) async-start(bf16[1,48,4,256]{3,1,0,2:T(8,128)(2,1)} %copy.23), calls=%async_computation.5 | async-start | bytes 196608 | tf_op jit(solution)/shard_map/all_to_all | solution.py:93
  40.7 25.1 %reduce-scatter.8.cloned.1.call-start = ((), (), s32[]{:S(2)}) async-start(), calls=%async_computation.10 | async-start | bytes 491520 | tf_op jit(solution)/shard_map/reduce_scatter | solution.py:46
  41.9 65.9 %reduce-scatter.16.cloned.1.call-start = ((), (), s32[]{:S(2)}) async-start(), calls=%async_computation.14 | async-start | bytes 983040 | tf_op jit(solution)/shard_map/reduce_scatter | solution.py:46
  65.7 56.6 %reduce-scatter.10.cloned.1.call-start = ((), (), s32[]{:S(2)}) async-start(), calls=%async_computation.11 | async-start | bytes 983040 | tf_op jit(solution)/shard_map/reduce_scatter | solution.py:46
  65.7 1.6 collective-permute-start
  101.6 45.6 %reduce-scatter.12.cloned.1.call-start = ((), (), s32[]{:S(2)}) async-start(), calls=%async_computation.12 | async-start | bytes 983040 | tf_op jit(solution)/shard_map/reduce_scatter | solution.py:46
  107.7 125.6 %reduce-scatter.18.cloned.1.call-start = ((), (), s32[]{:S(2)}) async-start(), calls=%async_computation.15 | async-start | bytes 884736 | tf_op jit(solution)/shard_map/reduce_scatter | solution.py:107
  198.4 107.1 %reduce-scatter.14.cloned.1.call-start = ((), (), s32[]{:S(2)}) async-start(), calls=%async_computation.13 | async-start | bytes 884736 | tf_op jit(solution)/shard_map/reduce_scatter | solution.py:107
  233.4 28.1 %collective-permute-start.2 = (bf16[48,1024]{1,0:T(8,128)(2,1)}, bf16[48,1024]{1,0:T(8,128)(2,1)S(1)}, u32[]{:S(2)}, u32[]{:S(2)}) collective-permute-start(bf16[48,1024]{1,0:T(8,128)(2,1)} %reduce-scatter.18.cloned.1.call-done), channel_id=1, source_target_pairs={{0,0},{1,1},{2,8},{3,9},{4,16},{5,17},{6,24},{7,25},{8,2},{9,3},{1... | collective-permute-start | bytes 294920 | tf_op jit(solution)/shard_map/ppermute | solution.py:56
  262.5 7.1 %collective-permute-start.3 = (bf16[48,1024]{1,0:T(8,128)(2,1)S(1)}, bf16[48,1024]{1,0:T(8,128)(2,1)S(1)}, u32[]{:S(2)}, u32[]{:S(2)}) collective-permute-start(bf16[48,1024]{1,0:T(8,128)(2,1)S(1)} %add_convert_fusion), channel_id=1, source_target_pairs={{0,8},{8,16},{16,24},{24,0},{1,9},{9,17},{17,25},{25,1},{2,10},{10... | collective-permute-start | bytes 294920 | tf_op jit(solution)/shard_map/ppermute | solution.py:130
  267.8 39.2 %copy-start.1 = (bf16[48,1024]{1,0:T(8,128)(2,1)S(1)}, bf16[48,1024]{1,0:T(8,128)(2,1)}, u32[]{:S(2)}) copy-start(bf16[48,1024]{1,0:T(8,128)(2,1)} %reduce-scatter.8.cloned.1.call-done) | copy-start | bytes 294916
  267.8 75.2 %copy-start.2 = (f32[2048]{0:T(1024)S(1)}, f32[2048]{0:T(1024)}, u32[]{:S(2)}) copy-start(f32[2048]{0:T(1024)} %param.10) | copy-start | bytes 24580
  267.8 76.0 %copy-start.3 = (s32[1,128]{1,0:T(1,128)S(1)}, s32[1,128]{1,0:T(1,128)}, u32[]{:S(2)}) copy-start(s32[1,128]{1,0:T(1,128)} %param.9) | copy-start | bytes 1540
  269.5 73.4 %reduce-scatter.20.cloned.1.call-start = ((), (), s32[]{:S(2)}) async-start(), calls=%async_computation.16 | async-start | bytes 294912 | tf_op jit(solution)/shard_map/reduce_scatter | solution.py:140
  269.6 6.8 %collective-permute-start.4 = (bf16[48,1024]{1,0:T(8,128)(2,1)S(1)}, bf16[48,1024]{1,0:T(8,128)(2,1)S(1)}, u32[]{:S(2)}, u32[]{:S(2)}) collective-permute-start(bf16[48,1024]{1,0:T(8,128)(2,1)S(1)} %collective-permute-done.3), channel_id=1, source_target_pairs={{0,8},{8,16},{16,24},{24,0},{1,9},{9,17},{17,25},{25,1},{2,10},{10... | collective-permute-start | bytes 294920 | tf_op jit(solution)/shard_map/ppermute | solution.py:130
  276.4 6.5 %collective-permute-start.5 = (bf16[48,1024]{1,0:T(8,128)(2,1)S(1)}, bf16[48,1024]{1,0:T(8,128)(2,1)S(1)}, u32[]{:S(2)}, u32[]{:S(2)}) collective-permute-start(bf16[48,1024]{1,0:T(8,128)(2,1)S(1)} %collective-permute-done.4), channel_id=1, source_target_pairs={{0,8},{8,16},{16,24},{24,0},{1,9},{9,17},{17,25},{25,1},{2,10},{10... | collective-permute-start | bytes 294920 | tf_op jit(solution)/shard_map/ppermute | solution.py:130
  305.5 1.5 collective-permute-start.1
Sparse Core Ops, SparseCore 0:
  44.4 21.0 reduce-scatter.7
  67.8 26.4 reduce-scatter.15
  101.7 20.5 reduce-scatter.9
  124.5 22.5 reduce-scatter.11
  198.5 34.8 reduce-scatter.17
  269.6 35.7 reduce-scatter.13
  309.4 33.5 reduce-scatter.19
